TPU v7x, 32 devices: a whole 2x2x4 slice. The times are simulated.
32 devices in a mesh: gx: 16 (over z, x, core), gy: 2 (over y).
Axes of the slice: x: 2, y: 2, z: 4, core: 2. Of those that a mesh axis runs over, the one named last changes fastest.
Arguments:
- volume_field: float32 [3, 256, 32, 128], P(None, 'gx', 'gy'), may hold values from -6 to 6
- diag_blocks: float32 [3, 3, 256, 32, 128], P(None, None, 'gx', 'gy'), may hold values from -4 to 4
- face_weights: float32 [6, 2, 256, 32, 128], P(None, None, 'gx', 'gy'), may hold values from 0.3 to 3
- boundary_field: float32 [16, 2, 1536], P('gx', 'gy'), may hold values from -6 to 6
- self_term: float32 [16, 2, 1536], P('gx', 'gy'), may hold values from 0.5 to 2
- coupling: float32 [16, 2, 1536], P('gx', 'gy'), may hold values from 0.3 to 3
- owner_map: int32 [16, 2, 1536], P('gx', 'gy'), may hold values from 0 to 1535, as said below
- left_basis: bfloat16 [32, 16, 2, 1536], P('gy', 'gx'), may hold values from -1 to 1
- right_basis: bfloat16 [256, 16, 2, 1536], P('gx', None, 'gy'), may hold values from -0.0390625 to 0.0390625
Outputs:
- volume_out: float32 [3, 256, 32, 128], P(None, 'gx', 'gy')
- boundary_out: float32 [16, 2, 1536], P('gx', 'gy')
Inputs may be any that keep to these rules, and one draw needn't show every extreme that they name: `owner_map`: within each subdomain (p, q) the 1536 entries name every surface edge of that subdomain exactly once.
All inputs are finite; a program needn't handle non-finite values.
Results may differ from a plain program's by a relative error of at most 0.0017.
Values may be sent and summed in bfloat16 or wider, within the bound.
No kernel may reach another device: no remote copies, remote signals or barrier semaphores. Data moves between devices by JAX's collectives and lax.ppermute only.
A program may use at most 64 MiB of HBM per device.

v0:
```python
import jax
import jax.numpy as jnp
from jax import lax
from jax.sharding import PartitionSpec as P


def with_halo(value, sides, width):
    for axis, dim in sides:
        devices, length = (lax.axis_size(axis), value.shape[dim])
        up = [(i, (i + 1) % devices) for i in range(devices - 1)]
        down = [(j, i) for i, j in up]
        last = lax.slice_in_dim(value, length - width, length, axis=dim)
        initial = lax.slice_in_dim(value, 0, width, axis=dim)
        before = lax.ppermute(last, axis, up)
        after = lax.ppermute(initial, axis, down)
        value = jnp.concatenate([before, value, after], axis=dim)
    return value


def apply_blocks(field_in, diag_blocks, face_weights, neighbours):
    comp_rows = []
    for comp in range(3):
        accum_row = (
            diag_blocks[comp, 0] * field_in[0]
            + diag_blocks[comp, 1] * field_in[1]
            + diag_blocks[comp, 2] * field_in[2]
        )
        comp_rows.append(accum_row)
    for offset in range(6):
        direction = offset // 2
        tangent = [comp for comp in range(3) if comp != direction]
        for slot in range(2):
            comp_rows[tangent[slot]] = (
                comp_rows[tangent[slot]] - face_weights[offset, slot] * neighbours[offset][slot]
            )
    return jnp.stack(comp_rows)


def on_device(
    volume_field,
    diag_blocks,
    face_weights,
    boundary_field,
    self_term,
    coupling,
    owner_map,
    left_basis,
    right_basis,
):
    z_padded = jnp.pad(volume_field[0:2], ((0, 0), (0, 0), (0, 0), (1, 1)))
    plus_z = z_padded[..., 2:]
    minus_z = z_padded[..., :-2]
    padded = with_halo(volume_field, (("gx", 1), ("gy", 2)), 1)
    plus_x = padded[1:3, 2:, 1:-1]
    minus_x = padded[1:3, :-2, 1:-1]
    plus_y = padded[0::2, 1:-1, 2:]
    minus_y = padded[0::2, 1:-1, :-2]
    neighbours = [plus_x, minus_x, plus_y, minus_y, plus_z, minus_z]
    stiffness = apply_blocks(volume_field, diag_blocks, face_weights, neighbours)
    cells_x = volume_field.shape[1]
    cells_y = volume_field.shape[2]
    boundary_count = boundary_field.shape[2]
    surface = jnp.stack([volume_field[..., 0], volume_field[..., -1]]).reshape(boundary_count)
    owner_flat = owner_map.reshape(boundary_count)
    edge_trace = surface[owner_flat].reshape(boundary_field.shape)
    placed = (
        jnp.zeros((boundary_count,), jnp.float32)
        .at[owner_flat]
        .set((coupling * boundary_field).reshape(boundary_count))
    )
    placed = placed.reshape(2, 3, cells_x, cells_y)
    volume_out = stiffness.at[:, :, :, 0].add(placed[0]).at[:, :, :, -1].add(placed[1])
    boundary_half = boundary_field.astype(jnp.bfloat16)
    gathered = lax.all_gather(boundary_half, "gx", axis=0, tiled=True)
    coef = jnp.einsum("rxbk,xbk->r", right_basis, gathered, preferred_element_type=jnp.float32)
    coef_half = coef.astype(jnp.bfloat16)
    partial_value = jnp.einsum(
        "rabk,r->abk", left_basis, coef_half, preferred_element_type=jnp.float32
    )
    integral = lax.psum_scatter(partial_value, "gy", scatter_dimension=1, tiled=True)
    boundary_out = self_term * boundary_field + integral + coupling * edge_trace
    return (volume_out, boundary_out)


def solution(mesh):
    return jax.shard_map(
        on_device,
        mesh=mesh,
        in_specs=(
            P(None, "gx", "gy", None),
            P(None, None, "gx", "gy", None),
            P(None, None, "gx", "gy", None),
            P("gx", "gy", None),
            P("gx", "gy", None),
            P("gx", "gy", None),
            P("gx", "gy", None),
            P("gy", "gx", None, None),
            P("gx", None, "gy", None),
        ),
        out_specs=(P(None, "gx", "gy", None), P("gx", "gy", None)),
        check_vma=False,
    )
```

profile of v0, /device:TPU:0, one launch (start us, length us, event | category | flops | bytes accessed | tf_op | source)
XLA Modules:
  0.0 75.5 jit_solution(9150187020478586098)
XLA Ops:
  0.7 1.4 %fusion.40 = (f32[3,1,16,128]{3,2,1,0:T(8,128)}, f32[3,1,16,128]{3,2,1,0:T(8,128)}) fusion(f32[3,16,16,128]{3,2,1,0:T(8,128)} %param.13), kind=kLoop, calls=%fused_computation.77 | loop fusion | bytes 98304 | tf_op jit(solution)/shard_map/slice | solution.py:13
  2.1 3.0 %collective-permute-start = (f32[3,1,16,128]{3,2,1,0:T(8,128)}, f32[3,1,16,128]{3,2,1,0:T(8,128)}, u32[]{:S(2)}, u32[]{:S(2)}) collective-permute-start(f32[3,1,16,128]{3,2,1,0:T(8,128)} %get-tuple-element.42), channel_id=1, source_target_pairs={{0,2},{2,4},{4,6},{6,8},{8,10},{10,12},{12,14},{14,16},{16,18},{18... | collective-permute-start | bytes 73736 | tf_op jit(solution)/shard_map/ppermute | solution.py:14
  5.1 1.3 %collective-permute-start.1 = (f32[3,1,16,128]{3,2,1,0:T(8,128)}, f32[3,1,16,128]{3,2,1,0:T(8,128)}, u32[]{:S(2)}, u32[]{:S(2)}) collective-permute-start(f32[3,1,16,128]{3,2,1,0:T(8,128)} %get-tuple-element.41), channel_id=1, source_target_pairs={{2,0},{4,2},{6,4},{8,6},{10,8},{12,10},{14,12},{16,14},{18,16},{20... | collective-permute-start | bytes 73736 | tf_op jit(solution)/shard_map/ppermute | solution.py:15
  6.4 1.3 %fusion.39 = (f32[3,16,16,1]{3,2,1,0:T(8,128)S(1)}, f32[3,16,16,1]{3,2,1,0:T(8,128)S(1)}) fusion(f32[3,16,16,128]{3,2,1,0:T(8,128)} %param.13), kind=kLoop, calls=%fused_computation.76 | loop fusion | bytes 12288 | tf_op jit(solution)/shard_map/slice | solution.py:63
  7.7 0.3 copy.61
  8.0 0.4 copy.62
  8.6 24.6 %all_gather.3 = bf16[16,1,1536]{2,1,0:T(2,128)(2,1)S(1)} all-gather(bf16[1,1,1536]{2,1,0:T(2,128)(2,1)S(1)} %convert_element_type.8), channel_id=1, replica_groups=mesh['gx'=16,'gy'=2] {'gx'}, dimensions={0}, use_global_device_ids=true | all-gather | bytes 52224 | tf_op jit(solution)/shard_map/all_gather | solution.py:74
  33.2 1.1 %fusion.4 = f32[1,2,1536]{2,0,1:T(1,128)S(1)} fusion(bf16[16,16,1536]{2,1,0:T(8,128)(2,1)S(1)} %bitcast.103, bf16[16,1,1536]{2,1,0:T(2,128)(2,1)S(1)} %all_gather.3, bf16[16,2,1536]{2,1,0:T(2,128)(2,1)S(1)} %bitcast.100), kind=kOutput, calls=%fused_computation.10 | convolution fusion | flops 884752 | bytes 946176 | tf_op jit(solution)/shard_map/rabk,r->abk/dot_general | solution.py:77
  34.4 8.1 %all-reduce.1 = f32[1,2,1536]{2,1,0:T(2,128)S(1)} all-reduce(f32[1,2,1536]{2,1,0:T(2,128)S(1)} %copy.58), channel_id=2, replica_groups=mesh['gx'=16,'gy'=2] {'gy'}, use_global_device_ids=true, to_apply=%region_1.2.clone | all-reduce | flops 3072 | bytes 24576
  42.5 8.4 %gather_fusion = f32[1536]{0:T(1024)S(1)} fusion(f32[1536]{0:T(1024)S(1)} %reshape.175, s32[2048]{0:T(1024)S(1)} %pad_clamp_fusion), kind=kCustom, calls=%fused_computation | custom fusion | bytes 18432 | tf_op jit(solution)/shard_map/gather | solution.py:65
  50.9 0.7 dynamic-slice.14
  51.6 1.3 %fusion.34 = (f32[1,1,1536]{2,1,0:T(1,128)}, f32[1536]{0:T(1024)S(1)}) fusion(f32[1,2,1536]{2,1,0:T(2,128)S(1)} %all-reduce.1, u32[]{:T(128)} %bitcast.32, f32[1,1,1536]{2,1,0:T(1,128)S(1)} %copy-done.6, f32[1536]{0:T(1024)S(1)} %gather_fusion, f32[1,1,1536]{2,1,0:T(1,128)S(1)} %copy-done.7, f32[1,1,1536]{2,1,0:T(1,128)S(1)} %copy-done.4), kind=kLoop, calls=%fused_computation.70 | loop fusion | flops 7680 | bytes 43012 | tf_op jit(solution)/shard_map/add | solution.py:81
  52.9 6.2 %scatter_custom_fusion = f32[1536]{0:T(1024)S(1)} fusion(s32[1536]{0:T(1024)S(1)} %fusion.33, f32[1536]{0:T(1024)S(1)} %get-tuple-element.48, f32[]{:T(128)} %constant.58.clone.1), kind=kCustom, calls=%fused_computation.72 | custom fusion | bytes 6148 | tf_op jit(solution)/shard_map/scatter | solution.py:69
  59.1 0.6 fusion.41
  59.8 0.8 reshape.171
  60.5 0.7 constant_dynamic-update-slice_fusion.6
  61.4 0.7 constant_dynamic-update-slice_fusion.3
  62.2 2.4 %collective-permute-start.2 = (f32[3,18,1,128]{3,2,1,0:T(1,128)S(1)}, f32[3,18,1,128]{3,2,1,0:T(1,128)S(1)}, u32[]{:S(2)}, u32[]{:S(2)}) collective-permute-start(f32[3,18,1,128]{3,2,1,0:T(1,128)S(1)} %get-tuple-element.34), channel_id=1, source_target_pairs={{0,1},{2,3},{4,5},{6,7},{8,9},{10,11},{12,13},{14,15},{16,17},{18,... | collective-permute-start | bytes 82952 | tf_op jit(solution)/shard_map/ppermute | solution.py:14
  64.6 1.3 %collective-permute-start.3 = (f32[3,18,1,128]{3,2,1,0:T(1,128)S(1)}, f32[3,18,1,128]{3,2,1,0:T(1,128)S(1)}, u32[]{:S(2)}, u32[]{:S(2)}) collective-permute-start(f32[3,18,1,128]{3,2,1,0:T(1,128)S(1)} %get-tuple-element.35), channel_id=1, source_target_pairs={{1,0},{3,2},{5,4},{7,6},{9,8},{11,10},{13,12},{15,14},{17,16},{19,... | collective-permute-start | bytes 82952 | tf_op jit(solution)/shard_map/ppermute | solution.py:15
  65.9 0.2 fusion.12
  66.1 4.2 %collective-permute-done.3 = f32[3,18,1,128]{3,2,1,0:T(1,128)S(1)} collective-permute-done((f32[3,18,1,128]{3,2,1,0:T(1,128)S(1)}, f32[3,18,1,128]{3,2,1,0:T(1,128)S(1)}, u32[]{:S(2)}, u32[]{:S(2)}) %collective-permute-start.3) | collective-permute-done | bytes 27680 | tf_op jit(solution)/shard_map/ppermute | solution.py:15
  70.8 0.8 %pad_maximum_fusion.1 = f32[3,16,16,128]{3,2,1,0:T(8,128)} fusion(f32[1,16,16,128]{3,2,1,0:T(8,128)S(1)} %fusion.14, f32[1,16,16,128]{3,2,1,0:T(8,128)S(1)} %fusion.12, f32[1,16,16,128]{3,2,1,0:T(8,128)S(1)} %fusion.8), kind=kLoop, calls=%fused_computation.12 | loop fusion | flops 196608 | bytes 786432 | tf_op jit(solution)/shard_map/stack | solution.py:36
  71.6 2.1 %copy.51 = f32[3,16,16,128]{2,1,0,3:T(8,128)S(1)} copy(f32[3,16,16,128]{3,2,1,0:T(8,128)} %pad_maximum_fusion.1) | data formatting | bytes 786432 | tf_op jit(solution)/shard_map/stack | solution.py:36
  73.7 1.8 %copy.54 = f32[3,16,16,128]{3,2,1,0:T(8,128)} copy(f32[3,16,16,128]{2,1,0,3:T(8,128)S(1)} %fusion.31) | data formatting | bytes 786432
  (39 shorter events, 0.9 us)
Async XLA Ops:
  0.6 32.6 %copy-start = (bf16[16,1,2,1536]{3,2,1,0:T(2,128)(2,1)S(1)}, bf16[16,1,2,1536]{3,2,1,0:T(2,128)(2,1)}, u32[]{:S(2)}) copy-start(bf16[16,1,2,1536]{3,2,1,0:T(2,128)(2,1)} %param.20) | copy-start | bytes 294916
  0.6 7.9 %copy-start.5 = (s32[1,1,1536]{2,1,0:T(1,128)S(1)}, s32[1,1,1536]{2,1,0:T(1,128)}, u32[]{:S(2)}) copy-start(s32[1,1,1536]{2,1,0:T(1,128)} %param.19) | copy-start | bytes 18436
  0.7 7.9 %copy-start.4 = (f32[1,1,1536]{2,1,0:T(1,128)S(1)}, f32[1,1,1536]{2,1,0:T(1,128)}, u32[]{:S(2)}) copy-start(f32[1,1,1536]{2,1,0:T(1,128)} %param.16) | copy-start | bytes 18436
  0.7 32.6 %copy-start.8 = (bf16[16,16,1,1536]{3,1,2,0:T(8,128)(2,1)S(1)}, bf16[16,16,1,1536]{3,1,2,0:T(8,128)(2,1)}, u32[]{:S(2)}) copy-start(bf16[16,16,1,1536]{3,1,2,0:T(8,128)(2,1)} %param.21) | copy-start | bytes 2359300
  2.1 58.4 %collective-permute-start = (f32[3,1,16,128]{3,2,1,0:T(8,128)}, f32[3,1,16,128]{3,2,1,0:T(8,128)}, u32[]{:S(2)}, u32[]{:S(2)}) collective-permute-start(f32[3,1,16,128]{3,2,1,0:T(8,128)} %get-tuple-element.42), channel_id=1, source_target_pairs={{0,2},{2,4},{4,6},{6,8},{8,10},{10,12},{12,14},{14,16},{16,18},{18... | collective-permute-start | bytes 73736 | tf_op jit(solution)/shard_map/ppermute | solution.py:14
  5.1 56.3 %collective-permute-start.1 = (f32[3,1,16,128]{3,2,1,0:T(8,128)}, f32[3,1,16,128]{3,2,1,0:T(8,128)}, u32[]{:S(2)}, u32[]{:S(2)}) collective-permute-start(f32[3,1,16,128]{3,2,1,0:T(8,128)} %get-tuple-element.41), channel_id=1, source_target_pairs={{2,0},{4,2},{6,4},{8,6},{10,8},{12,10},{14,12},{16,14},{18,16},{20... | collective-permute-start | bytes 73736 | tf_op jit(solution)/shard_map/ppermute | solution.py:15
  42.5 8.5 %copy-start.9 = (u32[32]{0:T(128)S(1)}, u32[32]{0:T(128)}, u32[]{:S(2)}) copy-start(u32[32]{0:T(128)} %constant.72) | copy-start | bytes 388
  42.5 9.1 %copy-start.6 = (f32[1,1,1536]{2,1,0:T(1,128)S(1)}, f32[1,1,1536]{2,1,0:T(1,128)}, u32[]{:S(2)}) copy-start(f32[1,1,1536]{2,1,0:T(1,128)} %param.18) | copy-start | bytes 18436
  42.5 9.1 %copy-start.7 = (f32[1,1,1536]{2,1,0:T(1,128)S(1)}, f32[1,1,1536]{2,1,0:T(1,128)}, u32[]{:S(2)}) copy-start(f32[1,1,1536]{2,1,0:T(1,128)} %param.17) | copy-start | bytes 18436
  42.5 17.2 %copy-start.1 = (f32[3,16,16,128]{3,2,1,0:T(8,128)S(1)}, f32[3,16,16,128]{3,2,1,0:T(8,128)}, u32[]{:S(2)}) copy-start(f32[3,16,16,128]{3,2,1,0:T(8,128)} %param.13) | copy-start | bytes 1179652
  42.5 23.4 %copy-start.3 = (f32[3,3,16,16,128]{4,3,2,1,0:T(8,128)S(1)}, f32[3,3,16,16,128]{4,3,2,1,0:T(8,128)}, u32[]{:S(2)}) copy-start(f32[3,3,16,16,128]{4,3,2,1,0:T(8,128)} %param.14) | copy-start | bytes 3538948
  50.9 15.0 %copy-start.2 = (f32[6,2,16,16,128]{4,3,2,1,0:T(8,128)S(1)}, f32[6,2,16,16,128]{4,3,2,1,0:T(8,128)}, u32[]{:S(2)}) copy-start(f32[6,2,16,16,128]{4,3,2,1,0:T(8,128)} %param.15) | copy-start | bytes 4718596
  62.2 4.0 %collective-permute-start.2 = (f32[3,18,1,128]{3,2,1,0:T(1,128)S(1)}, f32[3,18,1,128]{3,2,1,0:T(1,128)S(1)}, u32[]{:S(2)}, u32[]{:S(2)}) collective-permute-start(f32[3,18,1,128]{3,2,1,0:T(1,128)S(1)} %get-tuple-element.34), channel_id=1, source_target_pairs={{0,1},{2,3},{4,5},{6,7},{8,9},{10,11},{12,13},{14,15},{16,17},{18,... | collective-permute-start | bytes 82952 | tf_op jit(solution)/shard_map/ppermute | solution.py:14
  64.6 5.8 %collective-permute-start.3 = (f32[3,18,1,128]{3,2,1,0:T(1,128)S(1)}, f32[3,18,1,128]{3,2,1,0:T(1,128)S(1)}, u32[]{:S(2)}, u32[]{:S(2)}) collective-permute-start(f32[3,18,1,128]{3,2,1,0:T(1,128)S(1)} %get-tuple-element.35), channel_id=1, source_target_pairs={{1,0},{3,2},{5,4},{7,6},{9,8},{11,10},{13,12},{15,14},{17,16},{19,... | collective-permute-start | bytes 82952 | tf_op jit(solution)/shard_map/ppermute | solution.py:15
where the time goes:
time: 75.9 us; the launch traced here: 75.5 us
  blocking collectives  32.7 us (43%)
  local copies, waits for them, and re-layouts  25.7 us (34%)
  starting transfers between devices  7.98 us (11%)
  waiting for transfers between devices  4.27 us (6%)
  other arithmetic  2.72 us (4%)
  matrix products  1.12 us (1%)
  between operations  0.9 us (1%)
    all_gather x1, blocking collectives, on_device(): gathered = lax.all_gather(boundary_half, 'gx', axis=0, tiled=True)  24.6 us
    gather x1, local copies, waits for them, and re-layouts, on_device(): edge_trace = surface[owner_flat].reshape(boundary_field.shape)  8.39 us
    unnamed x1, blocking collectives  8.11 us
    scatter x1, local copies, waits for them, and re-layouts, on_device(): placed = jnp.zeros((boundary_count,), jnp.float32).at[owner_flat].set((co...  6.18 us
    ppermute x2, starting transfers between devices, with_halo(): before = lax.ppermute(last, axis, up)  5.41 us
    ppermute x2, waiting for transfers between devices, with_halo(): after = lax.ppermute(initial, axis, down)  4.23 us
    unnamed x26, local copies, waits for them, and re-layouts  4.02 us
    ppermute x2, starting transfers between devices, with_halo(): after = lax.ppermute(initial, axis, down)  2.57 us
  transfers between devices with their start and end apart: 4, of which 1 were waited for; matrix products, arithmetic and copies ran while one was open for 29% of the time, Pallas kernels for 0%

commit v1 on v0

--- a/solution.py
+++ b/solution.py
@@ -2,6 +2,16 @@
 import jax.numpy as jnp
 from jax import lax
 from jax.sharding import PartitionSpec as P
+
+
+def gather_by_hops(array, axis, dim):
+    count = lax.axis_size(axis)
+    held, blocks = (array, [array])
+    for _ in range(count - 1):
+        held = lax.ppermute(held, axis, [(i, (i + 1) % count) for i in range(count)])
+        blocks.insert(0, held)
+    flat = jnp.concatenate(blocks, axis=dim)
+    return jnp.roll(flat, (lax.axis_index(axis) + 1) * array.shape[dim], axis=dim)
 
 
 def with_halo(value, sides, width):
@@ -71,7 +81,7 @@
     placed = placed.reshape(2, 3, cells_x, cells_y)
     volume_out = stiffness.at[:, :, :, 0].add(placed[0]).at[:, :, :, -1].add(placed[1])
     boundary_half = boundary_field.astype(jnp.bfloat16)
-    gathered = lax.all_gather(boundary_half, "gx", axis=0, tiled=True)
+    gathered = gather_by_hops(boundary_half, "gx", 0)
     coef = jnp.einsum("rxbk,xbk->r", right_basis, gathered, preferred_element_type=jnp.float32)
     coef_half = coef.astype(jnp.bfloat16)
     partial_value = jnp.einsum(

time: 75.9 us -> 125 us (1.65)
  waiting for transfers between devices: 4.27 us -> 67 us
  blocking collectives: 32.7 us -> 9.76 us
  other arithmetic: 2.72 us -> 9.84 us
    ppermute x0 -> x15, waiting for transfers between devices: none -> 67 us  [gather_by_hops(): lax.ppermute(held, axis, [(i, (i + 1) % count) for i in range(count)])]
    all_gather x1 -> x0, blocking collectives: 24.6 us -> none  [on_device(): gathered = lax.all_gather(boundary_half, 'gx', axis=0, tiled=True)]
    ppermute x2, waiting for transfers between devices: 4.23 us -> 0.01 us  [with_halo(): after = lax.ppermute(initial, axis, down)]
    scatter-add x2, other arithmetic: 0.01 us -> 2.69 us  [on_device(): stiffness.at[:, :, :, 0].add(placed[0]).at[:, :, :, -1].add(placed[1])]
    sub x3, other arithmetic: 0.46 us -> 3.03 us  [apply_blocks(): comp_rows[tangent[slot]]]
    unnamed x26 -> x82, local copies, waits for them, and re-layouts: 4.02 us -> 5.79 us
    unnamed x1, blocking collectives: 8.11 us -> 9.76 us
  transfers between devices with their start and end apart: 4 -> 19, of which waited for: 1 -> 13; matrix products, arithmetic and copies ran while one was open for 29% -> 21% of each run, Pallas kernels for 0% -> 0%
where the time goes in v1:
time: 125 us
  waiting for transfers between devices  67 us (54%)
  local copies, waits for them, and re-layouts  25.8 us (21%)
  other arithmetic  9.84 us (8%)
  blocking collectives  9.76 us (8%)
  starting transfers between devices  8.98 us (7%)
  matrix products  2.16 us (2%)
    ppermute x15, waiting for transfers between devices, gather_by_hops(): lax.ppermute(held, axis, [(i, (i + 1) % count) for i in range(count)])  67 us
    unnamed x1, blocking collectives  9.76 us
    gather x1, local copies, waits for them, and re-layouts, on_device(): edge_trace = surface[owner_flat].reshape(boundary_field.shape)  8.39 us
    scatter x1, local copies, waits for them, and re-layouts, on_device(): placed = jnp.zeros((boundary_count,), jnp.float32).at[owner_flat].set((co...  6.18 us
    unnamed x82, local copies, waits for them, and re-layouts  5.79 us
    ppermute x2, starting transfers between devices, with_halo(): before = lax.ppermute(last, axis, up)  5.77 us
    sub x3, other arithmetic, apply_blocks(): comp_rows[tangent[slot]]  3.03 us
    scatter-add x2, other arithmetic, on_device(): stiffness.at[:, :, :, 0].add(placed[0]).at[:, :, :, -1].add(placed[1])  2.69 us
  transfers between devices with their start and end apart: 19, of which 13 were waited for; matrix products, arithmetic and copies ran while one was open for 21% of the time, Pallas kernels for 0%

profile of v1, /device:TPU:0, one launch (start us, length us, event | category | flops | bytes accessed | tf_op | source)
XLA Modules:
  0.0 124.8 jit_solution(4269798558740508668)
XLA Ops:
  2.0 6.3 %collective-permute-done.4 = bf16[1,1,1536]{2,1,0:T(2,128)(2,1)S(1)} collective-permute-done((bf16[1,1,1536]{2,1,0:T(2,128)(2,1)S(1)}, bf16[1,1,1536]{2,1,0:T(2,128)(2,1)S(1)}, u32[]{:S(2)}, u32[]{:S(2)}) %collective-permute-start.4) | collective-permute-done | bytes 3104 | tf_op jit(solution)/shard_map/ppermute | solution.py:11
  8.2 5.7 %collective-permute-done.5 = bf16[1,1,1536]{2,1,0:T(2,128)(2,1)S(1)} collective-permute-done((bf16[1,1,1536]{2,1,0:T(2,128)(2,1)S(1)}, bf16[1,1,1536]{2,1,0:T(2,128)(2,1)S(1)}, u32[]{:S(2)}, u32[]{:S(2)}) %collective-permute-start.5) | collective-permute-done | bytes 3104 | tf_op jit(solution)/shard_map/ppermute | solution.py:11
  14.0 5.7 %collective-permute-done.6 = bf16[1,1,1536]{2,1,0:T(2,128)(2,1)S(1)} collective-permute-done((bf16[1,1,1536]{2,1,0:T(2,128)(2,1)S(1)}, bf16[1,1,1536]{2,1,0:T(2,128)(2,1)S(1)}, u32[]{:S(2)}, u32[]{:S(2)}) %collective-permute-start.6) | collective-permute-done | bytes 3104 | tf_op jit(solution)/shard_map/ppermute | solution.py:11
  19.7 5.7 %collective-permute-done.7 = bf16[1,1,1536]{2,1,0:T(2,128)(2,1)S(1)} collective-permute-done((bf16[1,1,1536]{2,1,0:T(2,128)(2,1)S(1)}, bf16[1,1,1536]{2,1,0:T(2,128)(2,1)S(1)}, u32[]{:S(2)}, u32[]{:S(2)}) %collective-permute-start.7) | collective-permute-done | bytes 3104 | tf_op jit(solution)/shard_map/ppermute | solution.py:11
  25.5 5.7 %collective-permute-done.8 = bf16[1,1,1536]{2,1,0:T(2,128)(2,1)S(1)} collective-permute-done((bf16[1,1,1536]{2,1,0:T(2,128)(2,1)S(1)}, bf16[1,1,1536]{2,1,0:T(2,128)(2,1)S(1)}, u32[]{:S(2)}, u32[]{:S(2)}) %collective-permute-start.8) | collective-permute-done | bytes 3104 | tf_op jit(solution)/shard_map/ppermute | solution.py:11
  34.6 2.4 %collective-permute-done.9 = bf16[1,1,1536]{2,1,0:T(2,128)(2,1)S(1)} collective-permute-done((bf16[1,1,1536]{2,1,0:T(2,128)(2,1)S(1)}, bf16[1,1,1536]{2,1,0:T(2,128)(2,1)S(1)}, u32[]{:S(2)}, u32[]{:S(2)}) %collective-permute-start.9) | collective-permute-done | bytes 3104 | tf_op jit(solution)/shard_map/ppermute | solution.py:11
  37.0 1.4 %fusion.43 = (f32[3,16,16,1]{3,2,1,0:T(8,128)S(1)}, f32[3,16,16,1]{3,2,1,0:T(8,128)S(1)}) fusion(f32[3,16,16,128]{3,2,1,0:T(8,128)} %param.13), kind=kLoop, calls=%fused_computation.110 | loop fusion | bytes 12288 | tf_op jit(solution)/shard_map/slice | solution.py:73
  38.4 4.4 %collective-permute-done.10 = bf16[1,1,1536]{2,1,0:T(2,128)(2,1)S(1)} collective-permute-done((bf16[1,1,1536]{2,1,0:T(2,128)(2,1)S(1)}, bf16[1,1,1536]{2,1,0:T(2,128)(2,1)S(1)}, u32[]{:S(2)}, u32[]{:S(2)}) %collective-permute-start.10) | collective-permute-done | bytes 3104 | tf_op jit(solution)/shard_map/ppermute | solution.py:11
  43.5 5.0 %collective-permute-done.11 = bf16[1,1,1536]{2,1,0:T(2,128)(2,1)S(1)} collective-permute-done((bf16[1,1,1536]{2,1,0:T(2,128)(2,1)S(1)}, bf16[1,1,1536]{2,1,0:T(2,128)(2,1)S(1)}, u32[]{:S(2)}, u32[]{:S(2)}) %collective-permute-start.11) | collective-permute-done | bytes 3104 | tf_op jit(solution)/shard_map/ppermute | solution.py:11
  48.6 5.7 %collective-permute-done.12 = bf16[1,1,1536]{2,1,0:T(2,128)(2,1)S(1)} collective-permute-done((bf16[1,1,1536]{2,1,0:T(2,128)(2,1)S(1)}, bf16[1,1,1536]{2,1,0:T(2,128)(2,1)S(1)}, u32[]{:S(2)}, u32[]{:S(2)}) %collective-permute-start.12) | collective-permute-done | bytes 3104 | tf_op jit(solution)/shard_map/ppermute | solution.py:11
  54.5 8.4 %gather_fusion = f32[1536]{0:T(1024)S(1)} fusion(f32[1536]{0:T(1024)S(1)} %reshape.175, s32[2048]{0:T(1024)S(1)} %pad_clamp_fusion), kind=kCustom, calls=%fused_computation | custom fusion | bytes 18432 | tf_op jit(solution)/shard_map/gather | solution.py:75
  63.6 5.7 %collective-permute-done.14 = bf16[1,1,1536]{2,1,0:T(2,128)(2,1)S(1)} collective-permute-done((bf16[1,1,1536]{2,1,0:T(2,128)(2,1)S(1)}, bf16[1,1,1536]{2,1,0:T(2,128)(2,1)S(1)}, u32[]{:S(2)}, u32[]{:S(2)}) %collective-permute-start.14) | collective-permute-done | bytes 3104 | tf_op jit(solution)/shard_map/ppermute | solution.py:11
  69.5 5.6 %collective-permute-done.15 = bf16[1,1,1536]{2,1,0:T(2,128)(2,1)S(1)} collective-permute-done((bf16[1,1,1536]{2,1,0:T(2,128)(2,1)S(1)}, bf16[1,1,1536]{2,1,0:T(2,128)(2,1)S(1)}, u32[]{:S(2)}, u32[]{:S(2)}) %collective-permute-start.15) | collective-permute-done | bytes 3104 | tf_op jit(solution)/shard_map/ppermute | solution.py:11
  75.9 5.0 %collective-permute-done.16 = bf16[1,1,1536]{2,1,0:T(2,128)(2,1)S(1)} collective-permute-done((bf16[1,1,1536]{2,1,0:T(2,128)(2,1)S(1)}, bf16[1,1,1536]{2,1,0:T(2,128)(2,1)S(1)}, u32[]{:S(2)}, u32[]{:S(2)}) %collective-permute-start.16) | collective-permute-done | bytes 3104 | tf_op jit(solution)/shard_map/ppermute | solution.py:11
  80.9 4.5 %collective-permute-start.2 = (f32[3,18,1,128]{3,2,1,0:T(1,128)S(1)}, f32[3,18,1,128]{3,2,1,0:T(1,128)}, u32[]{:S(2)}, u32[]{:S(2)}) collective-permute-start(f32[3,18,1,128]{3,2,1,0:T(1,128)S(1)} %get-tuple-element.32), channel_id=1, source_target_pairs={{0,1},{2,3},{4,5},{6,7},{8,9},{10,11},{12,13},{14,15},{16,17},{18,... | collective-permute-start | bytes 82952 | tf_op jit(solution)/shard_map/ppermute | solution.py:24
  86.8 1.8 %fusion.12 = f32[1,16,16,128]{3,2,1,0:T(8,128)} fusion(f32[2,16,16,128]{3,2,1,0:T(8,128)S(1)} %slice.250, f32[3,17,16,128]{3,2,1,0:T(8,128)S(1)} %get-tuple-element.38, f32[3,17,16,128]{3,2,1,0:T(8,128)S(1)} %get-tuple-element.41, f32[6,2,16,16,128]{4,3,2,1,0:T(8,128)S(1)} %copy-done.2, f32[3,3,16,16,128]{4,3,2,1,0:T(8,128)} %param.14, ...), kind=kLoop, calls=%fused_computation.19 | loop fusion | flops 425984 | bytes 1966080 | tf_op jit(solution)/shard_map/sub | solution.py:44
  88.6 3.9 %collective-permute-done.18 = bf16[1,1,1536]{2,1,0:T(2,128)(2,1)S(1)} collective-permute-done((bf16[1,1,1536]{2,1,0:T(2,128)(2,1)S(1)}, bf16[1,1,1536]{2,1,0:T(2,128)(2,1)S(1)}, u32[]{:S(2)}, u32[]{:S(2)}) %collective-permute-start.18) | collective-permute-done | bytes 3104 | tf_op jit(solution)/shard_map/ppermute | solution.py:11
  93.9 2.2 %fusion.4 = f32[1,2,1536]{2,0,1:T(1,128)S(1)} fusion(bf16[16,16,1536]{2,1,0:T(8,128)(2,1)S(1)} %bitcast.100, bf16[16,2,1536]{2,1,0:T(2,128)(2,1)} %bitcast.103, bf16[32,1,1536]{2,1,0:T(2,128)(2,1)} %copy-done.21, s32[]{:T(128)S(6)} %select_n.26), kind=kOutput, calls=%fused_computation.10 | convolution fusion | flops 884752 | bytes 995332 | tf_op jit(solution)/shard_map/rabk,r->abk/dot_general | solution.py:87
  96.1 9.8 %all-reduce.1 = f32[1,2,1536]{2,1,0:T(2,128)S(1)} all-reduce(f32[1,2,1536]{2,1,0:T(2,128)S(1)} %copy.53), channel_id=2, replica_groups=mesh['gx'=16,'gy'=2] {'gy'}, use_global_device_ids=true, to_apply=%region_1.2.clone | all-reduce | flops 3072 | bytes 24576
  105.8 2.0 %fusion.36 = (f32[1,1,1536]{2,1,0:T(1,128)}, f32[1536]{0:T(1024)S(1)}) fusion(f32[1,2,1536]{2,1,0:T(2,128)S(1)} %all-reduce.1, u32[]{:T(128)} %bitcast.32, f32[1,1,1536]{2,1,0:T(1,128)} %param.18, f32[1536]{0:T(1024)S(1)} %gather_fusion, f32[1,1,1536]{2,1,0:T(1,128)} %param.17, f32[1,1,1536]{2,1,0:T(1,128)S(1)} %copy-done.7), kind=kLoop, calls=%fused_computation.103 | loop fusion | flops 7680 | bytes 43012 | tf_op jit(solution)/shard_map/add | solution.py:91
  107.8 6.2 %scatter_custom_fusion = f32[1536]{0:T(1024)S(1)} fusion(s32[1536]{0:T(1024)S(1)} %fusion.35, f32[1536]{0:T(1024)S(1)} %get-tuple-element.46, f32[]{:T(128)} %constant.81.clone.1), kind=kCustom, calls=%fused_computation.105 | custom fusion | bytes 6148 | tf_op jit(solution)/shard_map/scatter | solution.py:79
  116.9 2.2 %copy.46 = f32[3,16,16,128]{2,1,0,3:T(8,128)} copy(f32[3,16,16,128]{3,2,1,0:T(8,128)S(1)} %pad_maximum_fusion.1) | data formatting | bytes 786432 | tf_op jit(solution)/shard_map/stack | solution.py:46
  120.4 1.3 %fusion.33 = f32[3,16,16,128]{2,1,0,3:T(8,128)} fusion(f32[3,16,16,128]{2,1,0,3:T(8,128)} %fusion.34, f32[3,16,16,1]{2,1,0,3:T(8,128)S(1)} %reshape.171), kind=kLoop, calls=%fused_computation.97 | loop fusion | flops 768 | bytes 52224 | tf_op jit(solution)/shard_map/scatter-add | solution.py:82
  121.8 3.0 %copy.49 = f32[3,16,16,128]{3,2,1,0:T(8,128)} copy(f32[3,16,16,128]{2,1,0,3:T(8,128)} %fusion.33) | data formatting | bytes 786432
  (126 shorter events, 13.8 us)
Async XLA Ops:
  0.6 92.6 %copy-start = (bf16[16,16,1,1536]{3,1,2,0:T(8,128)(2,1)S(1)}, bf16[16,16,1,1536]{3,1,2,0:T(8,128)(2,1)}, u32[]{:S(2)}) copy-start(bf16[16,16,1,1536]{3,1,2,0:T(8,128)(2,1)} %param.21) | copy-start | bytes 2359300
  0.6 53.7 %copy-start.1 = (f32[3,16,16,128]{3,2,1,0:T(8,128)S(1)}, f32[3,16,16,128]{3,2,1,0:T(8,128)}, u32[]{:S(2)}) copy-start(f32[3,16,16,128]{3,2,1,0:T(8,128)} %param.13) | copy-start | bytes 1179652
  0.7 42.1 %copy-start.20 = (s32[1,1,1536]{2,1,0:T(1,128)S(1)}, s32[1,1,1536]{2,1,0:T(1,128)}, u32[]{:S(2)}) copy-start(s32[1,1,1536]{2,1,0:T(1,128)} %param.19) | copy-start | bytes 18436
  1.5 6.8 %collective-permute-start.4 = (bf16[1,1,1536]{2,1,0:T(2,128)(2,1)S(1)}, bf16[1,1,1536]{2,1,0:T(2,128)(2,1)S(1)}, u32[]{:S(2)}, u32[]{:S(2)}) collective-permute-start(bf16[1,1,1536]{2,1,0:T(2,128)(2,1)S(1)} %convert_element_type.8), channel_id=1, source_target_pairs={{0,2},{2,4},{4,6},{6,8},{8,10},{10,12},{12,14},{14,16},{16,18},{18... | collective-permute-start | bytes 9224 | tf_op jit(solution)/shard_map/ppermute | solution.py:11
  8.2 5.8 %collective-permute-start.5 = (bf16[1,1,1536]{2,1,0:T(2,128)(2,1)S(1)}, bf16[1,1,1536]{2,1,0:T(2,128)(2,1)S(1)}, u32[]{:S(2)}, u32[]{:S(2)}) collective-permute-start(bf16[1,1,1536]{2,1,0:T(2,128)(2,1)S(1)} %collective-permute-done.4), channel_id=1, source_target_pairs={{0,2},{2,4},{4,6},{6,8},{8,10},{10,12},{12,14},{14,16},{16,18},{18... | collective-permute-start | bytes 9224 | tf_op jit(solution)/shard_map/ppermute | solution.py:11
  14.0 5.8 %collective-permute-start.6 = (bf16[1,1,1536]{2,1,0:T(2,128)(2,1)S(1)}, bf16[1,1,1536]{2,1,0:T(2,128)(2,1)S(1)}, u32[]{:S(2)}, u32[]{:S(2)}) collective-permute-start(bf16[1,1,1536]{2,1,0:T(2,128)(2,1)S(1)} %collective-permute-done.5), channel_id=1, source_target_pairs={{0,2},{2,4},{4,6},{6,8},{8,10},{10,12},{12,14},{14,16},{16,18},{18... | collective-permute-start | bytes 9224 | tf_op jit(solution)/shard_map/ppermute | solution.py:11
  19.7 5.8 %collective-permute-start.7 = (bf16[1,1,1536]{2,1,0:T(2,128)(2,1)S(1)}, bf16[1,1,1536]{2,1,0:T(2,128)(2,1)S(1)}, u32[]{:S(2)}, u32[]{:S(2)}) collective-permute-start(bf16[1,1,1536]{2,1,0:T(2,128)(2,1)S(1)} %collective-permute-done.6), channel_id=1, source_target_pairs={{0,2},{2,4},{4,6},{6,8},{8,10},{10,12},{12,14},{14,16},{16,18},{18... | collective-permute-start | bytes 9224 | tf_op jit(solution)/shard_map/ppermute | solution.py:11
  25.5 5.8 %collective-permute-start.8 = (bf16[1,1,1536]{2,1,0:T(2,128)(2,1)S(1)}, bf16[1,1,1536]{2,1,0:T(2,128)(2,1)S(1)}, u32[]{:S(2)}, u32[]{:S(2)}) collective-permute-start(bf16[1,1,1536]{2,1,0:T(2,128)(2,1)S(1)} %collective-permute-done.7), channel_id=1, source_target_pairs={{0,2},{2,4},{4,6},{6,8},{8,10},{10,12},{12,14},{14,16},{16,18},{18... | collective-permute-start | bytes 9224 | tf_op jit(solution)/shard_map/ppermute | solution.py:11
  31.2 5.8 %collective-permute-start.9 = (bf16[1,1,1536]{2,1,0:T(2,128)(2,1)S(1)}, bf16[1,1,1536]{2,1,0:T(2,128)(2,1)S(1)}, u32[]{:S(2)}, u32[]{:S(2)}) collective-permute-start(bf16[1,1,1536]{2,1,0:T(2,128)(2,1)S(1)} %collective-permute-done.8), channel_id=1, source_target_pairs={{0,2},{2,4},{4,6},{6,8},{8,10},{10,12},{12,14},{14,16},{16,18},{18... | collective-permute-start | bytes 9224 | tf_op jit(solution)/shard_map/ppermute | solution.py:11
  32.0 31.6 %collective-permute-start = (f32[3,1,16,128]{3,2,1,0:T(8,128)S(1)}, f32[3,1,16,128]{3,2,1,0:T(8,128)S(1)}, u32[]{:S(2)}, u32[]{:S(2)}) collective-permute-start(f32[3,1,16,128]{3,2,1,0:T(8,128)S(1)} %get-tuple-element.40), channel_id=1, source_target_pairs={{0,2},{2,4},{4,6},{6,8},{8,10},{10,12},{12,14},{14,16},{16,18},{18... | collective-permute-start | bytes 73736 | tf_op jit(solution)/shard_map/ppermute | solution.py:24
  33.3 41.8 %collective-permute-start.1 = (f32[3,1,16,128]{3,2,1,0:T(8,128)S(1)}, f32[3,1,16,128]{3,2,1,0:T(8,128)}, u32[]{:S(2)}, u32[]{:S(2)}) collective-permute-start(f32[3,1,16,128]{3,2,1,0:T(8,128)S(1)} %get-tuple-element.39), channel_id=1, source_target_pairs={{2,0},{4,2},{6,4},{8,6},{10,8},{12,10},{14,12},{16,14},{18,16},{20... | collective-permute-start | bytes 73736 | tf_op jit(solution)/shard_map/ppermute | solution.py:25
  37.0 5.8 %collective-permute-start.10 = (bf16[1,1,1536]{2,1,0:T(2,128)(2,1)S(1)}, bf16[1,1,1536]{2,1,0:T(2,128)(2,1)S(1)}, u32[]{:S(2)}, u32[]{:S(2)}) collective-permute-start(bf16[1,1,1536]{2,1,0:T(2,128)(2,1)S(1)} %collective-permute-done.9), channel_id=1, source_target_pairs={{0,2},{2,4},{4,6},{6,8},{8,10},{10,12},{12,14},{14,16},{16,18},{18... | collective-permute-start | bytes 9224 | tf_op jit(solution)/shard_map/ppermute | solution.py:11
  42.7 5.8 %collective-permute-start.11 = (bf16[1,1,1536]{2,1,0:T(2,128)(2,1)S(1)}, bf16[1,1,1536]{2,1,0:T(2,128)(2,1)S(1)}, u32[]{:S(2)}, u32[]{:S(2)}) collective-permute-start(bf16[1,1,1536]{2,1,0:T(2,128)(2,1)S(1)} %collective-permute-done.10), channel_id=1, source_target_pairs={{0,2},{2,4},{4,6},{6,8},{8,10},{10,12},{12,14},{14,16},{16,18},{18... | collective-permute-start | bytes 9224 | tf_op jit(solution)/shard_map/ppermute | solution.py:11
  48.5 5.8 %collective-permute-start.12 = (bf16[1,1,1536]{2,1,0:T(2,128)(2,1)S(1)}, bf16[1,1,1536]{2,1,0:T(2,128)(2,1)S(1)}, u32[]{:S(2)}, u32[]{:S(2)}) collective-permute-start(bf16[1,1,1536]{2,1,0:T(2,128)(2,1)S(1)} %collective-permute-done.11), channel_id=1, source_target_pairs={{0,2},{2,4},{4,6},{6,8},{8,10},{10,12},{12,14},{14,16},{16,18},{18... | collective-permute-start | bytes 9224 | tf_op jit(solution)/shard_map/ppermute | solution.py:11
  54.3 9.3 %collective-permute-start.13 = (bf16[1,1,1536]{2,1,0:T(2,128)(2,1)S(1)}, bf16[1,1,1536]{2,1,0:T(2,128)(2,1)S(1)}, u32[]{:S(2)}, u32[]{:S(2)}) collective-permute-start(bf16[1,1,1536]{2,1,0:T(2,128)(2,1)S(1)} %collective-permute-done.12), channel_id=1, source_target_pairs={{0,2},{2,4},{4,6},{6,8},{8,10},{10,12},{12,14},{14,16},{16,18},{18... | collective-permute-start | bytes 9224 | tf_op jit(solution)/shard_map/ppermute | solution.py:11
  62.9 23.9 %copy-start.2 = (f32[6,2,16,16,128]{4,3,2,1,0:T(8,128)S(1)}, f32[6,2,16,16,128]{4,3,2,1,0:T(8,128)}, u32[]{:S(2)}) copy-start(f32[6,2,16,16,128]{4,3,2,1,0:T(8,128)} %param.15) | copy-start | bytes 4718596
  63.6 5.8 %collective-permute-start.14 = (bf16[1,1,1536]{2,1,0:T(2,128)(2,1)S(1)}, bf16[1,1,1536]{2,1,0:T(2,128)(2,1)S(1)}, u32[]{:S(2)}, u32[]{:S(2)}) collective-permute-start(bf16[1,1,1536]{2,1,0:T(2,128)(2,1)S(1)} %collective-permute-done.13), channel_id=1, source_target_pairs={{0,2},{2,4},{4,6},{6,8},{8,10},{10,12},{12,14},{14,16},{16,18},{18... | collective-permute-start | bytes 9224 | tf_op jit(solution)/shard_map/ppermute | solution.py:11
  69.3 5.8 %collective-permute-start.15 = (bf16[1,1,1536]{2,1,0:T(2,128)(2,1)S(1)}, bf16[1,1,1536]{2,1,0:T(2,128)(2,1)S(1)}, u32[]{:S(2)}, u32[]{:S(2)}) collective-permute-start(bf16[1,1,1536]{2,1,0:T(2,128)(2,1)S(1)} %collective-permute-done.14), channel_id=1, source_target_pairs={{0,2},{2,4},{4,6},{6,8},{8,10},{10,12},{12,14},{14,16},{16,18},{18... | collective-permute-start | bytes 9224 | tf_op jit(solution)/shard_map/ppermute | solution.py:11
  69.4 23.5 %copy-start.7 = (f32[1,1,1536]{2,1,0:T(1,128)S(1)}, f32[1,1,1536]{2,1,0:T(1,128)}, u32[]{:S(2)}) copy-start(f32[1,1,1536]{2,1,0:T(1,128)} %param.16) | copy-start | bytes 18436
  75.1 5.8 %collective-permute-start.16 = (bf16[1,1,1536]{2,1,0:T(2,128)(2,1)S(1)}, bf16[1,1,1536]{2,1,0:T(2,128)(2,1)S(1)}, u32[]{:S(2)}, u32[]{:S(2)}) collective-permute-start(bf16[1,1,1536]{2,1,0:T(2,128)(2,1)S(1)} %collective-permute-done.15), channel_id=1, source_target_pairs={{0,2},{2,4},{4,6},{6,8},{8,10},{10,12},{12,14},{14,16},{16,18},{18... | collective-permute-start | bytes 9224 | tf_op jit(solution)/shard_map/ppermute | solution.py:11
  80.9 5.9 %collective-permute-start.17 = (bf16[1,1,1536]{2,1,0:T(2,128)(2,1)S(1)}, bf16[1,1,1536]{2,1,0:T(2,128)(2,1)S(1)}, u32[]{:S(2)}, u32[]{:S(2)}) collective-permute-start(bf16[1,1,1536]{2,1,0:T(2,128)(2,1)S(1)} %collective-permute-done.16), channel_id=1, source_target_pairs={{0,2},{2,4},{4,6},{6,8},{8,10},{10,12},{12,14},{14,16},{16,18},{18... | collective-permute-start | bytes 9224 | tf_op jit(solution)/shard_map/ppermute | solution.py:11
  80.9 33.3 %collective-permute-start.2 = (f32[3,18,1,128]{3,2,1,0:T(1,128)S(1)}, f32[3,18,1,128]{3,2,1,0:T(1,128)}, u32[]{:S(2)}, u32[]{:S(2)}) collective-permute-start(f32[3,18,1,128]{3,2,1,0:T(1,128)S(1)} %get-tuple-element.32), channel_id=1, source_target_pairs={{0,1},{2,3},{4,5},{6,7},{8,9},{10,11},{12,13},{14,15},{16,17},{18,... | collective-permute-start | bytes 82952 | tf_op jit(solution)/shard_map/ppermute | solution.py:24
  85.4 28.8 %collective-permute-start.3 = (f32[3,18,1,128]{3,2,1,0:T(1,128)S(1)}, f32[3,18,1,128]{3,2,1,0:T(1,128)}, u32[]{:S(2)}, u32[]{:S(2)}) collective-permute-start(f32[3,18,1,128]{3,2,1,0:T(1,128)S(1)} %get-tuple-element.33), channel_id=1, source_target_pairs={{1,0},{3,2},{5,4},{7,6},{9,8},{11,10},{13,12},{15,14},{17,16},{19,... | collective-permute-start | bytes 82952 | tf_op jit(solution)/shard_map/ppermute | solution.py:25
  86.7 5.8 %collective-permute-start.18 = (bf16[1,1,1536]{2,1,0:T(2,128)(2,1)S(1)}, bf16[1,1,1536]{2,1,0:T(2,128)(2,1)S(1)}, u32[]{:S(2)}, u32[]{:S(2)}) collective-permute-start(bf16[1,1,1536]{2,1,0:T(2,128)(2,1)S(1)} %collective-permute-done.17), channel_id=1, source_target_pairs={{0,2},{2,4},{4,6},{6,8},{8,10},{10,12},{12,14},{14,16},{16,18},{18... | collective-permute-start | bytes 9224 | tf_op jit(solution)/shard_map/ppermute | solution.py:11
  (18 other events, 240.1 us)
